TPU v7x, 32 devices: a whole 2x2x4 slice. The times are simulated.
32 devices in a mesh: dp: 8 (over z, y), sp: 4 (over x, core).
Axes of the slice: x: 2, y: 2, z: 4, core: 2. Of those that a mesh axis runs over, the one named last changes fastest.
Arguments:
- tokens: bfloat16 [16, 1024, 512], P('dp', 'sp'), may hold values from -6 to 6
- lengths: int32 [16], P('dp'), may hold values from 64 to 1024, as said below
- post_query: bfloat16 [512, 512], replicated, may hold values from -0.25 to 0.25
- post_key: bfloat16 [512, 512], replicated, may hold values from -0.25 to 0.25
- post_value: bfloat16 [512, 512], replicated, may hold values from -0.25 to 0.25
- post_out: bfloat16 [512, 512], replicated, may hold values from -1 to 1
- post_gate: bfloat16 [512, 1376], replicated, may hold values from -0.25 to 0.25
- post_up: bfloat16 [512, 1376], replicated, may hold values from -0.25 to 0.25
- post_down: bfloat16 [1376, 512], replicated, may hold values from -0.15625 to 0.15625
- post_attn_gain: float32 [512], replicated, may hold values from 0.5 to 1.5
- post_ffn_gain: float32 [512], replicated, may hold values from 0.5 to 1.5
- pre_query: bfloat16 [512, 512], replicated, may hold values from -0.25 to 0.25
- pre_key: bfloat16 [512, 512], replicated, may hold values from -0.25 to 0.25
- pre_value: bfloat16 [512, 512], replicated, may hold values from -0.25 to 0.25
- pre_out: bfloat16 [512, 512], replicated, may hold values from -1 to 1
- pre_gate: bfloat16 [512, 1376], replicated, may hold values from -0.25 to 0.25
- pre_up: bfloat16 [512, 1376], replicated, may hold values from -0.25 to 0.25
- pre_down: bfloat16 [1376, 512], replicated, may hold values from -0.15625 to 0.15625
- pre_attn_gain: float32 [512], replicated, may hold values from 0.5 to 1.5
- pre_ffn_gain: float32 [512], replicated, may hold values from 0.5 to 1.5
- out_grad: bfloat16 [16, 1024, 512], P('dp', 'sp'), may hold values from -6 to 6
Outputs:
- output: bfloat16 [16, 1024, 512], P('dp', 'sp')
- tokens_grad: bfloat16 [16, 1024, 512], P('dp', 'sp')
- grad_post_query: float32 [512, 512], replicated
- grad_post_key: float32 [512, 512], replicated
- grad_post_value: float32 [512, 512], replicated
- grad_post_out: float32 [512, 512], replicated
- grad_post_gate: float32 [512, 1376], replicated
- grad_post_up: float32 [512, 1376], replicated
- grad_post_down: float32 [1376, 512], replicated
- grad_post_attn_gain: float32 [512], replicated
- grad_post_ffn_gain: float32 [512], replicated
- grad_pre_query: float32 [512, 512], replicated
- grad_pre_key: float32 [512, 512], replicated
- grad_pre_value: float32 [512, 512], replicated
- grad_pre_out: float32 [512, 512], replicated
- grad_pre_gate: float32 [512, 1376], replicated
- grad_pre_up: float32 [512, 1376], replicated
- grad_pre_down: float32 [1376, 512], replicated
- grad_pre_attn_gain: float32 [512], replicated
- grad_pre_ffn_gain: float32 [512], replicated
Inputs may be any that keep to these rules, and one draw needn't show every extreme that they name: `lengths`: some slot has length exactly 1024 and some exactly 64.
All inputs are finite; a program needn't handle non-finite values.
Results may differ from a plain program's by a relative error of at most 0.024.
Values may be sent and summed in bfloat16 or wider, within the bound.
No kernel may reach another device: no remote copies, remote signals or barrier semaphores. Data moves between devices by JAX's collectives and lax.ppermute only.
A program may use at most 192 MiB of HBM per device.

v0:
```python
import jax
import jax.numpy as jnp
from jax import lax
from jax.sharding import PartitionSpec as P

HEADS = 8
HD = 64
SEQ = 1024
eps = 1e-06


def norm_rows(values, gain_vec):
    return values * lax.rsqrt(jnp.mean(values * values, axis=-1, keepdims=True) + eps) * gain_vec


def rotary_tables(start, row_count):
    half_dim = HD // 2
    inverse = 10000.0 ** (-jnp.arange(half_dim, dtype=jnp.float32) * 2.0 / HD)
    positions = (start + jnp.arange(row_count, dtype=jnp.int32)).astype(jnp.float32)
    angles = positions[:, None] * inverse[None, :]
    cosine = jnp.concatenate([jnp.cos(angles), jnp.cos(angles)], axis=-1)
    sine_table = jnp.concatenate([jnp.sin(angles), jnp.sin(angles)], axis=-1)
    return (cosine, sine_table)


def rotate(values, cosine, sine_table):
    half_dim = values.shape[-1] // 2
    turned = jnp.concatenate([-values[..., half_dim:], values[..., :half_dim]], axis=-1)
    return values * cosine[:, None, :] + turned * sine_table[:, None, :]


def rotate_back(grads, cosine, sine_table):
    half_dim = grads.shape[-1] // 2
    turned = grads * sine_table[:, None, :]
    backward = jnp.concatenate([turned[..., half_dim:], -turned[..., :half_dim]], axis=-1)
    return grads * cosine[:, None, :] + backward


def gated(gate_act, up_act):
    return jax.nn.silu(gate_act) * up_act


def slot_scores(queries, key_heads, length):
    scores = jnp.einsum(
        "qhd,khd->hqk", queries, key_heads, preferred_element_type=jnp.float32
    ) * HD ** (-0.5)
    row_index = jnp.arange(SEQ, dtype=jnp.int32)[:, None]
    col_index = jnp.arange(SEQ, dtype=jnp.int32)[None, :]
    allowed = (col_index <= row_index) & (col_index < length)
    return jnp.where(allowed[None], scores, -1000000000.0)


def attend_slot(pieces):
    queries, key_heads, value_heads, length = pieces
    scores = slot_scores(queries, key_heads, length)
    maxima = jnp.max(scores, axis=-1, keepdims=True)
    log_total = maxima + jnp.log(jnp.sum(jnp.exp(scores - maxima), axis=-1, keepdims=True))
    softmax_p = jnp.exp(scores - log_total)
    mixed_heads = jnp.einsum(
        "hqk,khd->qhd",
        softmax_p.astype(jnp.bfloat16),
        value_heads,
        preferred_element_type=jnp.float32,
    )
    return (mixed_heads.astype(jnp.bfloat16), log_total)


def attend_back(pieces):
    queries, key_heads, value_heads, log_total, grad_mixed, length = pieces
    softmax_p = jnp.exp(slot_scores(queries, key_heads, length) - log_total)
    grad_values = jnp.einsum(
        "hqk,qhd->khd",
        softmax_p.astype(jnp.bfloat16),
        grad_mixed,
        preferred_element_type=jnp.float32,
    )
    grad_probs = jnp.einsum(
        "qhd,khd->hqk", grad_mixed, value_heads, preferred_element_type=jnp.float32
    )
    row_delta = jnp.sum(softmax_p * grad_probs, axis=-1, keepdims=True)
    grad_scores = (softmax_p * (grad_probs - row_delta)).astype(jnp.bfloat16)
    grad_queries = jnp.einsum(
        "hqk,khd->qhd", grad_scores, key_heads, preferred_element_type=jnp.float32
    ) * HD ** (-0.5)
    grad_keys = jnp.einsum(
        "hqk,qhd->khd", grad_scores, queries, preferred_element_type=jnp.float32
    ) * HD ** (-0.5)
    return (
        grad_queries.astype(jnp.bfloat16),
        grad_keys.astype(jnp.bfloat16),
        grad_values.astype(jnp.bfloat16),
    )


def layer_forward(inputs, weights, lengths, post_norm, cosine, sine_table):
    w_query, w_key, w_value, w_out, w_gate, w_up, w_down, gain_att, gain_ffn = weights
    group = lax.axis_size("sp")
    slot_count, row_count, width = inputs.shape
    local_heads = HEADS // group
    full_rows = row_count * group
    if post_norm:
        entry_rows = inputs.astype(jnp.bfloat16)
    else:
        entry_rows = norm_rows(inputs, gain_att).astype(jnp.bfloat16)

    def rotated(weight):
        product = jnp.einsum("nsd,de->nse", entry_rows, weight, preferred_element_type=jnp.float32)
        turned = rotate(product.reshape(slot_count, row_count, HEADS, HD), cosine, sine_table)
        return turned.astype(jnp.bfloat16).reshape(slot_count, row_count, group, local_heads * HD)

    query_rows = rotated(w_query)
    key_rows = rotated(w_key)
    value_rows = jnp.einsum("nsd,de->nse", entry_rows, w_value, preferred_element_type=jnp.float32)
    value_rows = value_rows.astype(jnp.bfloat16).reshape(
        slot_count, row_count, group, local_heads * HD
    )
    query_heads, key_heads, value_heads = (
        lax.all_to_all(query_rows, "sp", split_axis=2, concat_axis=1, tiled=True),
        lax.all_to_all(key_rows, "sp", split_axis=2, concat_axis=1, tiled=True),
        lax.all_to_all(value_rows, "sp", split_axis=2, concat_axis=1, tiled=True),
    )

    def head_view(values):
        return values.reshape(slot_count, full_rows, local_heads, HD)

    query_heads = head_view(query_heads)
    key_heads = head_view(key_heads)
    value_heads = head_view(value_heads)
    mixed_heads, log_total = lax.map(attend_slot, (query_heads, key_heads, value_heads, lengths))
    mixed_rows = lax.all_to_all(
        mixed_heads.reshape(slot_count, full_rows, 1, local_heads * HD),
        "sp",
        split_axis=1,
        concat_axis=2,
        tiled=True,
    )
    mixed_rows = mixed_rows.reshape(slot_count, row_count, width)
    middle = inputs + jnp.einsum(
        "nsd,de->nse", mixed_rows, w_out, preferred_element_type=jnp.float32
    )
    if post_norm:
        state_rows = norm_rows(middle, gain_att)
        ffn_in = state_rows.astype(jnp.bfloat16)
    else:
        state_rows = middle
        ffn_in = norm_rows(middle, gain_ffn).astype(jnp.bfloat16)
    gate_act = jnp.einsum("nsd,df->nsf", ffn_in, w_gate, preferred_element_type=jnp.float32)
    up_act = jnp.einsum("nsd,df->nsf", ffn_in, w_up, preferred_element_type=jnp.float32)
    hidden = gated(gate_act, up_act).astype(jnp.bfloat16)
    result = state_rows + jnp.einsum(
        "nsf,fd->nsd", hidden, w_down, preferred_element_type=jnp.float32
    )
    saved = (
        inputs,
        entry_rows,
        query_heads,
        key_heads,
        value_heads,
        log_total,
        mixed_rows,
        middle,
        ffn_in,
        gate_act,
        up_act,
        hidden,
        result,
    )
    if post_norm:
        return (norm_rows(result, gain_ffn), saved)
    return (result, saved)


def layer_backward(grad_output, saved, weights, lengths, post_norm, cosine, sine_table):
    w_query, w_key, w_value, w_out, w_gate, w_up, w_down, gain_att, gain_ffn = weights
    (
        inputs,
        entry_rows,
        query_heads,
        key_heads,
        value_heads,
        log_total,
        mixed_rows,
        middle,
        ffn_in,
        gate_act,
        up_act,
        hidden,
        result,
    ) = saved
    group = lax.axis_size("sp")
    slot_count, row_count, width = inputs.shape
    local_heads = HEADS // group
    full_rows = row_count * group
    if post_norm:
        discard, pull_result = jax.vjp(norm_rows, result, gain_ffn)
        grad_result, grad_gain_ffn = pull_result(grad_output)
    else:
        grad_result = grad_output
    grad_down_in = grad_result.astype(jnp.bfloat16)
    grad_w_down = jnp.einsum(
        "nsf,nsd->fd", hidden, grad_down_in, preferred_element_type=jnp.float32
    )
    grad_hidden = jnp.einsum(
        "nsd,fd->nsf", grad_down_in, w_down, preferred_element_type=jnp.float32
    )
    discard, pull_glu = jax.vjp(gated, gate_act, up_act)
    grad_gate, grad_up = pull_glu(grad_hidden)
    grad_gate = grad_gate.astype(jnp.bfloat16)
    grad_up = grad_up.astype(jnp.bfloat16)
    grad_w_gate = jnp.einsum("nsd,nsf->df", ffn_in, grad_gate, preferred_element_type=jnp.float32)
    grad_w_up = jnp.einsum("nsd,nsf->df", ffn_in, grad_up, preferred_element_type=jnp.float32)
    grad_ffn_in = jnp.einsum("nsf,df->nsd", grad_gate, w_gate, preferred_element_type=jnp.float32)
    grad_ffn_in = grad_ffn_in + jnp.einsum(
        "nsf,df->nsd", grad_up, w_up, preferred_element_type=jnp.float32
    )
    if post_norm:
        discard, pull_middle = jax.vjp(norm_rows, middle, gain_att)
        grad_middle, grad_gain_att = pull_middle(grad_result + grad_ffn_in)
    else:
        discard, pull_middle = jax.vjp(norm_rows, middle, gain_ffn)
        grad_normed, grad_gain_ffn = pull_middle(grad_ffn_in)
        grad_middle = grad_result + grad_normed
    grad_attn = grad_middle.astype(jnp.bfloat16)
    grad_w_out = jnp.einsum(
        "nsd,nse->de", mixed_rows, grad_attn, preferred_element_type=jnp.float32
    )
    grad_mixed = jnp.einsum(
        "nse,de->nsd", grad_attn, w_out, preferred_element_type=jnp.float32
    ).astype(jnp.bfloat16)
    grad_mixed = lax.all_to_all(
        grad_mixed.reshape(slot_count, row_count, group, local_heads * HD),
        "sp",
        split_axis=2,
        concat_axis=1,
        tiled=True,
    )
    grad_mixed = grad_mixed.reshape(slot_count, full_rows, local_heads, HD)
    grad_queries, grad_keys, grad_values = lax.map(
        attend_back, (query_heads, key_heads, value_heads, log_total, grad_mixed, lengths)
    )

    def head_pack(values):
        return values.reshape(slot_count, full_rows, 1, local_heads * HD)

    grad_query_rows, grad_key_rows, grad_value_rows = (
        lax.all_to_all(head_pack(grad_queries), "sp", split_axis=1, concat_axis=2, tiled=True),
        lax.all_to_all(head_pack(grad_keys), "sp", split_axis=1, concat_axis=2, tiled=True),
        lax.all_to_all(head_pack(grad_values), "sp", split_axis=1, concat_axis=2, tiled=True),
    )

    def unrotate(values):
        grads = values.astype(jnp.float32).reshape(slot_count, row_count, HEADS, HD)
        return (
            rotate_back(grads, cosine, sine_table)
            .astype(jnp.bfloat16)
            .reshape(slot_count, row_count, width)
        )

    grad_query_pre = unrotate(grad_query_rows)
    grad_key_pre = unrotate(grad_key_rows)
    grad_value_pre = grad_value_rows.reshape(slot_count, row_count, width)
    grad_w_query = jnp.einsum(
        "nsd,nse->de", entry_rows, grad_query_pre, preferred_element_type=jnp.float32
    )
    grad_w_key = jnp.einsum(
        "nsd,nse->de", entry_rows, grad_key_pre, preferred_element_type=jnp.float32
    )
    grad_w_value = jnp.einsum(
        "nsd,nse->de", entry_rows, grad_value_pre, preferred_element_type=jnp.float32
    )
    grad_entry = jnp.einsum(
        "nse,de->nsd", grad_query_pre, w_query, preferred_element_type=jnp.float32
    )
    grad_entry = grad_entry + jnp.einsum(
        "nse,de->nsd", grad_key_pre, w_key, preferred_element_type=jnp.float32
    )
    grad_entry = grad_entry + jnp.einsum(
        "nse,de->nsd", grad_value_pre, w_value, preferred_element_type=jnp.float32
    )
    if post_norm:
        grad_inputs = grad_middle + grad_entry
    else:
        discard, pull_inputs = jax.vjp(norm_rows, inputs, gain_att)
        grad_normed_in, grad_gain_att = pull_inputs(grad_entry)
        grad_inputs = grad_middle + grad_normed_in
    return (
        grad_inputs,
        (
            grad_w_query,
            grad_w_key,
            grad_w_value,
            grad_w_out,
            grad_w_gate,
            grad_w_up,
            grad_w_down,
            grad_gain_att,
            grad_gain_ffn,
        ),
    )


def reduce_grads(grads):
    weights = tuple((grad.astype(jnp.bfloat16) for grad in grads[:7]))
    summed = lax.psum(weights, ("dp", "sp"))
    gains = lax.psum(grads[7:], ("dp", "sp"))
    return tuple((grad.astype(jnp.float32) for grad in summed)) + tuple(gains)


def body(
    tokens,
    lengths,
    post_query,
    post_key,
    post_value,
    post_out,
    post_gate,
    post_up,
    post_down,
    post_attn_gain,
    post_ffn_gain,
    pre_query,
    pre_key,
    pre_value,
    pre_out,
    pre_gate,
    pre_up,
    pre_down,
    pre_attn_gain,
    pre_ffn_gain,
    out_grad,
):
    slot_count, row_count, width = tokens.shape
    start = lax.axis_index("sp") * row_count
    cosine, sine_table = rotary_tables(start, row_count)
    layer_one = (
        post_query,
        post_key,
        post_value,
        post_out,
        post_gate,
        post_up,
        post_down,
        post_attn_gain,
        post_ffn_gain,
    )
    layer_two = (
        pre_query,
        pre_key,
        pre_value,
        pre_out,
        pre_gate,
        pre_up,
        pre_down,
        pre_attn_gain,
        pre_ffn_gain,
    )
    inputs_one = tokens.astype(jnp.float32)
    middle_state, saved_one = layer_forward(
        inputs_one, layer_one, lengths, True, cosine, sine_table
    )
    final_state, saved_two = layer_forward(
        middle_state, layer_two, lengths, False, cosine, sine_table
    )
    output = final_state.astype(jnp.bfloat16)
    positions = start + jnp.arange(row_count, dtype=jnp.int32)
    valid_rows = (positions[None, :] < lengths[:, None]).astype(jnp.float32)
    grad_final = out_grad.astype(jnp.float32) * valid_rows[:, :, None]
    grad_middle_state, grads_two = layer_backward(
        grad_final, saved_two, layer_two, lengths, False, cosine, sine_table
    )
    grad_tokens, grads_one = layer_backward(
        grad_middle_state, saved_one, layer_one, lengths, True, cosine, sine_table
    )
    grads_one = reduce_grads(grads_one)
    grads_two = reduce_grads(grads_two)
    tokens_grad = grad_tokens.astype(jnp.bfloat16)
    return (
        output,
        tokens_grad,
        grads_one[0],
        grads_one[1],
        grads_one[2],
        grads_one[3],
        grads_one[4],
        grads_one[5],
        grads_one[6],
        grads_one[7],
        grads_one[8],
        grads_two[0],
        grads_two[1],
        grads_two[2],
        grads_two[3],
        grads_two[4],
        grads_two[5],
        grads_two[6],
        grads_two[7],
        grads_two[8],
    )


def solution(mesh):
    in_specs = (
        P("dp", "sp", None),
        P("dp"),
        P(),
        P(),
        P(),
        P(),
        P(),
        P(),
        P(),
        P(),
        P(),
        P(),
        P(),
        P(),
        P(),
        P(),
        P(),
        P(),
        P(),
        P(),
        P("dp", "sp", None),
    )
    out_specs = (
        P("dp", "sp", None),
        P("dp", "sp", None),
        P(),
        P(),
        P(),
        P(),
        P(),
        P(),
        P(),
        P(),
        P(),
        P(),
        P(),
        P(),
        P(),
        P(),
        P(),
        P(),
        P(),
        P(),
    )
    return jax.shard_map(body, mesh=mesh, in_specs=in_specs, out_specs=out_specs, check_vma=False)
```

profile of v0, /device:TPU:0, one launch (start us, length us, event | category | flops | bytes accessed | tf_op | source)
XLA Modules:
  0.0 970.4 jit_solution(17261309546535177547)
XLA Ops:
  9.9 4.2 all-to-all-start
  19.5 4.1 all-to-all-done
  23.6 3.5 all-to-all-start.1
  27.9 8.0 all-to-all-done.1
  35.9 3.5 all-to-all-start.2
  51.6 17.7 %while.52 = (s32[]{:T(128)}, bf16[2,1024,2,64]{1,3,2,0:T(8,128)(2,1)}, f32[2,2,1024,1]{2,1,3,0:T(2,128)S(1)}, bf16[2,1024,2,64]{1,3,2,0:T(8,128)(2,1)}, s32[2]{0...) while((s32[]{:T(128)}, ...), condition=%wide.region_3.4_spmd, body=%wide.region_0.3_spmd.sunk | while | flops 562166784 | bytes 36769988 | solution.py:129
  71.6 12.7 %all_to_all.216 = bf16[2,1024,1,128]{3,0,2,1:T(2,128)(2,1)S(1)} all-to-all(bf16[2,1024,1,128]{3,0,2,1:T(2,128)(2,1)} %copy.321), channel_id=1, replica_groups=mesh['dp'=8,'sp'=4] {'sp'}, dimensions={1} | all-to-all | bytes 1048576 | tf_op jit(solution)/shard_map/all_to_all | solution.py:130
  91.7 2.8 multiply_convert_fusion.5
  98.1 4.1 all-to-all-start.4
  107.9 3.3 all-to-all-done.4
  111.2 3.5 all-to-all-start.5
  115.5 8.0 all-to-all-done.5
  123.5 3.6 all-to-all-start.6
  139.4 17.7 %while.53 = (s32[]{:T(128)}, bf16[2,1024,2,64]{1,3,2,0:T(8,128)(2,1)}, f32[2,2,1024,1]{2,1,3,0:T(2,128)S(1)}, bf16[2,1024,2,64]{1,3,2,0:T(8,128)(2,1)}, s32[2]{0...) while((s32[]{:T(128)}, ...), condition=%wide.region_10.11_spmd, body=%wide.region_7.10_spmd.sunk | while | flops 562166784 | bytes 36769988 | solution.py:129
  159.1 4.4 all-to-all-start.7
  163.5 4.1 fusion.136
  167.6 4.7 all-to-all-done.7
  180.9 3.0 fusion.130
  189.1 4.5 all-to-all-start.8
  193.7 3.4 fusion.126
  197.1 5.4 all-to-all-done.8
  209.4 28.9 %while.54 = (s32[]{:T(128)}, bf16[2,1024,2,64]{1,3,2,0:T(8,128)(2,1)}, bf16[2,1024,2,64]{1,3,2,0:T(8,128)(2,1)}, bf16[2,1024,2,64]{1,3,2,0:T(8,128)(2,1)}, bf16[...) while((s32[]{:T(128)}, ...), condition=%wide.region_15.16_spmd, body=%wide.region_13.15_spmd.sunk | while | flops 1376386048 | bytes 86572392 | solution.py:238
  212.4 3.0 multiply_reduce_fusion.16
  215.4 2.7 multiply_convert_fusion.11
  226.8 3.0 multiply_reduce_fusion.16
  229.8 2.7 multiply_convert_fusion.11
  240.3 3.6 all-to-all-start.10
  244.0 3.6 fusion.127
  247.6 3.2 fusion.123
  252.8 4.1 all-to-all-start.9
  262.9 2.9 all-to-all-done.9
  265.8 4.1 all-to-all-start.11
  272.2 2.5 copy.341
  302.6 4.4 all-to-all-start.12
  308.3 3.3 fusion.125
  311.6 4.2 all-to-all-done.12
  322.7 29.0 %while.55 = (s32[]{:T(128)}, bf16[2,1024,2,64]{1,3,2,0:T(8,128)(2,1)}, bf16[2,1024,2,64]{1,3,2,0:T(8,128)(2,1)}, bf16[2,1024,2,64]{1,3,2,0:T(8,128)(2,1)}, bf16[...) while((s32[]{:T(128)}, ...), condition=%wide.region_21.22_spmd, body=%wide.region_19.21_spmd.sunk | while | flops 1376386048 | bytes 86572392 | solution.py:238
  325.7 3.0 multiply_reduce_fusion.17
  328.7 2.7 multiply_convert_fusion.12
  340.2 3.0 multiply_reduce_fusion.17
  343.2 2.7 multiply_convert_fusion.12
  353.7 3.7 all-to-all-start.14
  359.8 3.6 fusion.122
  366.2 3.5 all-to-all-start.13
  379.3 3.5 all-to-all-start.15
  401.9 3.6 fusion.185
  405.5 42.8 %all-reduce = (f32[512]{0:T(512)}, f32[512]{0:T(512)}, f32[512]{0:T(512)}, f32[512]{0:T(512)}) all-reduce(f32[512]{0:T(512)S(1)} %get-tuple-element.339, f32[512]{0:T(512)S(1)} %get-tuple-element.334, f32[512]{0:T(512)S(1)} %get-tuple-element.336, f32[512]{0:T(512)S(1)} %copy-done.113), channel_id=1, replica_groups=mesh['dp'=8,'sp'=4] {'dp','sp'}, use_global_device_ids=true, to_apply=%region_30.31 | all-reduce | flops 2048 | bytes 16384 | tf_op jit(solution)/shard_map/psum | solution.py:305
  452.7 487.4 %all-reduce.4.cloned.1.call-done = (bf16[512,512]{0,1:T(8,128)(2,1)}, bf16[512,512]{0,1:T(8,128)(2,1)}, bf16[512,512]{0,1:T(8,128)(2,1)}, bf16[512,512]{1,0:T(8,...) async-done(((bf16[512,512]{0,1:T(8,128)(2,1)}, ...) | async-done | bytes 12648464 | tf_op jit(solution)/shard_map/psum | solution.py:304
  (512 shorter events, 255.8 us)
Async XLA Ops:
  7.2 172.5 %copy-start = (bf16[512,1376]{0,1:T(8,128)(2,1)S(1)}, bf16[512,1376]{0,1:T(8,128)(2,1)}, u32[]{:S(2)}) copy-start(bf16[512,1376]{0,1:T(8,128)(2,1)} %param.44) | copy-start | bytes 4227076
  7.2 6.9 copy-start.6
  7.2 8.7 copy-start.74
  9.9 13.7 %all-to-all-start = ((bf16[2,256,4,128]{3,1,0,2:T(8,128)(2,1)}), bf16[2,256,4,128]{3,1,0,2:T(8,128)(2,1)}, u32[]{:S(2)}, u32[]{:S(2)}) async-start(bf16[2,256,4,128]{3,1,0,2:T(8,128)(2,1)} %bitcast.512), calls=%async_computation | async-start | bytes 1048576 | tf_op jit(solution)/shard_map/all_to_all | solution.py:120
  16.9 88.8 %copy-start.12 = (f32[256,8,64]{0,2,1:T(8,128)}, f32[256,8,64]{0,2,1:T(8,128)S(1)}, u32[]{:S(2)}) copy-start(f32[256,8,64]{0,2,1:T(8,128)S(1)} %mul.485) | copy-start | bytes 1572868
  23.6 12.3 %all-to-all-start.1 = ((bf16[2,256,4,128]{1,3,0,2:T(8,128)(2,1)}), bf16[2,256,4,128]{1,3,0,2:T(8,128)(2,1)S(1)}, u32[]{:S(2)}, u32[]{:S(2)}) async-start(bf16[2,256,4,128]{1,3,0,2:T(8,128)(2,1)} %copy.315), calls=%async_computation.1 | async-start | bytes 1048576 | tf_op jit(solution)/shard_map/all_to_all | solution.py:118
  35.9 12.3 %all-to-all-start.2 = ((bf16[2,256,4,128]{1,3,0,2:T(8,128)(2,1)}), bf16[2,256,4,128]{1,3,0,2:T(8,128)(2,1)S(1)}, u32[]{:S(2)}, u32[]{:S(2)}) async-start(bf16[2,256,4,128]{1,3,0,2:T(8,128)(2,1)} %copy.319), calls=%async_computation.2 | async-start | bytes 1048576 | tf_op jit(solution)/shard_map/all_to_all | solution.py:119
  41.4 10.2 %copy-start.114 = (s32[2]{0:T(128)S(1)}, s32[2]{0:T(128)}, u32[]{:S(2)}) copy-start(s32[2]{0:T(128)} %param.30) | copy-start | bytes 28
  69.3 20.2 %copy-start.2 = (bf16[2,1024,2,64]{1,3,2,0:T(8,128)(2,1)}, bf16[2,1024,2,64]{1,3,2,0:T(8,128)(2,1)S(1)}, u32[]{:S(2)}) copy-start(bf16[2,1024,2,64]{1,3,2,0:T(8,128)(2,1)S(1)} %get-tuple-element.864) | copy-start | bytes 1572868
  69.3 20.2 %copy-start.8 = (bf16[2,1024,2,64]{1,3,2,0:T(8,128)(2,1)}, bf16[2,1024,2,64]{1,3,2,0:T(8,128)(2,1)S(1)}, u32[]{:S(2)}) copy-start(bf16[2,1024,2,64]{1,3,2,0:T(8,128)(2,1)S(1)} %get-tuple-element.866) | copy-start | bytes 1572868
  69.3 20.2 %copy-start.95 = (f32[2,2,1024,1]{2,1,3,0:T(2,128)}, f32[2,2,1024,1]{2,1,3,0:T(2,128)S(1)}, u32[]{:S(2)}) copy-start(f32[2,2,1024,1]{2,1,3,0:T(2,128)S(1)} %get-tuple-element.810) | copy-start | bytes 49156
  84.3 5.8 copy-start.104
  96.5 7.3 copy-start.106
  96.5 7.3 copy-start.102
  96.8 7.0 copy-start.4
  98.1 13.1 %all-to-all-start.4 = ((bf16[2,256,4,128]{3,1,0,2:T(8,128)(2,1)}), bf16[2,256,4,128]{3,1,0,2:T(8,128)(2,1)}, u32[]{:S(2)}, u32[]{:S(2)}) async-start(bf16[2,256,4,128]{3,1,0,2:T(8,128)(2,1)} %bitcast.625), calls=%async_computation.4 | async-start | bytes 1048576 | tf_op jit(solution)/shard_map/all_to_all | solution.py:120
  111.2 12.3 %all-to-all-start.5 = ((bf16[2,256,4,128]{1,3,0,2:T(8,128)(2,1)}), bf16[2,256,4,128]{1,3,0,2:T(8,128)(2,1)S(1)}, u32[]{:S(2)}, u32[]{:S(2)}) async-start(bf16[2,256,4,128]{1,3,0,2:T(8,128)(2,1)} %copy.328), calls=%async_computation.5 | async-start | bytes 1048576 | tf_op jit(solution)/shard_map/all_to_all | solution.py:118
  123.5 12.4 %all-to-all-start.6 = ((bf16[2,256,4,128]{1,3,0,2:T(8,128)(2,1)}), bf16[2,256,4,128]{1,3,0,2:T(8,128)(2,1)S(1)}, u32[]{:S(2)}, u32[]{:S(2)}) async-start(bf16[2,256,4,128]{1,3,0,2:T(8,128)(2,1)} %copy.332), calls=%async_computation.6 | async-start | bytes 1048576 | tf_op jit(solution)/shard_map/all_to_all | solution.py:119
  159.1 13.3 %all-to-all-start.7 = ((bf16[2,1024,1,128]{3,0,2,1:T(2,128)(2,1)}), bf16[2,1024,1,128]{3,0,2,1:T(2,128)(2,1)}, u32[]{:S(2)}, u32[]{:S(2)}) async-start(bf16[2,1024,1,128]{3,0,2,1:T(2,128)(2,1)} %copy.334), calls=%async_computation.7 | async-start | bytes 1048576 | tf_op jit(solution)/shard_map/all_to_all | solution.py:130
  178.5 8.2 copy-start.14
  178.8 5.1 copy-start.47
  189.1 13.4 %all-to-all-start.8 = ((bf16[2,256,4,128]{3,1,0,2:T(8,128)(2,1)}), bf16[2,256,4,128]{3,1,0,2:T(8,128)(2,1)}, u32[]{:S(2)}, u32[]{:S(2)}) async-start(bf16[2,256,4,128]{3,1,0,2:T(8,128)(2,1)} %bitcast.638), calls=%async_computation.8 | async-start | bytes 1048576 | tf_op jit(solution)/shard_map/all_to_all | solution.py:230
  240.3 12.4 %all-to-all-start.10 = ((bf16[2,1024,1,128]{3,0,2,1:T(2,128)(2,1)}), bf16[2,1024,1,128]{3,0,2,1:T(2,128)(2,1)S(1)}, u32[]{:S(2)}, u32[]{:S(2)}) async-start(bf16[2,1024,1,128]{3,0,2,1:T(2,128)(2,1)} %copy.344), calls=%async_computation.10 | async-start | bytes 1048576 | tf_op jit(solution)/shard_map/all_to_all | solution.py:247
  247.6 9.4 copy-start.34
  252.8 13.1 %all-to-all-start.9 = ((bf16[2,1024,1,128]{3,0,2,1:T(2,128)(2,1)}), bf16[2,1024,1,128]{3,0,2,1:T(2,128)(2,1)}, u32[]{:S(2)}, u32[]{:S(2)}) async-start(bf16[2,1024,1,128]{3,0,2,1:T(2,128)(2,1)} %copy.339), calls=%async_computation.9 | async-start | bytes 1048576 | tf_op jit(solution)/shard_map/all_to_all | solution.py:246
  262.9 11.8 %copy-start.18 = (f32[2,256,4,1,128]{1,4,2,0,3:T(8,128)}, f32[2,256,4,1,128]{1,4,2,0,3:T(8,128)S(1)}, u32[]{:S(2)}) copy-start(f32[2,256,4,1,128]{1,4,2,0,3:T(8,128)S(1)} %copy.346) | copy-start | bytes 3145732
  262.9 11.8 %copy-start.87 = (f32[256,64]{0,1:T(8,128)S(1)}, f32[256,64]{0,1:T(8,128)}, u32[]{:S(2)}) copy-start(f32[256,64]{0,1:T(8,128)} %copy-done.86) | copy-start | bytes 196612
  265.8 14.7 %all-to-all-start.11 = ((bf16[2,1024,1,128]{3,0,2,1:T(2,128)(2,1)}), bf16[2,1024,1,128]{3,0,2,1:T(2,128)(2,1)}, u32[]{:S(2)}, u32[]{:S(2)}) async-start(bf16[2,1024,1,128]{3,0,2,1:T(2,128)(2,1)} %copy.349), calls=%async_computation.11 | async-start | bytes 1048576 | tf_op jit(solution)/shard_map/all_to_all | solution.py:248
  278.3 8.6 copy-start.35
  281.6 5.2 copy-start.101
  289.0 5.5 copy-start.40
  299.7 7.2 copy-start.5
  299.7 7.3 copy-start.37
  302.6 13.3 %all-to-all-start.12 = ((bf16[2,256,4,128]{3,1,0,2:T(8,128)(2,1)}), bf16[2,256,4,128]{3,1,0,2:T(8,128)(2,1)}, u32[]{:S(2)}, u32[]{:S(2)}) async-start(bf16[2,256,4,128]{3,1,0,2:T(8,128)(2,1)} %bitcast.630), calls=%async_computation.12 | async-start | bytes 1048576 | tf_op jit(solution)/shard_map/all_to_all | solution.py:230
  311.6 11.1 %copy-start.3 = (bf16[2,1024,2,64]{1,3,2,0:T(8,128)(2,1)S(1)}, bf16[2,1024,2,64]{1,3,2,0:T(8,128)(2,1)}, u32[]{:S(2)}) copy-start(bf16[2,1024,2,64]{1,3,2,0:T(8,128)(2,1)} %copy-done.2) | copy-start | bytes 1572868
  311.6 11.1 %copy-start.9 = (bf16[2,1024,2,64]{1,3,2,0:T(8,128)(2,1)S(1)}, bf16[2,1024,2,64]{1,3,2,0:T(8,128)(2,1)}, u32[]{:S(2)}) copy-start(bf16[2,1024,2,64]{1,3,2,0:T(8,128)(2,1)} %copy-done.8) | copy-start | bytes 1572868
  311.6 11.1 %copy-start.96 = (f32[2,2,1024,1]{2,1,3,0:T(2,128)S(1)}, f32[2,2,1024,1]{2,1,3,0:T(2,128)}, u32[]{:S(2)}) copy-start(f32[2,2,1024,1]{2,1,3,0:T(2,128)} %copy-done.95) | copy-start | bytes 49156
  353.7 12.5 %all-to-all-start.14 = ((bf16[2,1024,1,128]{3,0,2,1:T(2,128)(2,1)}), bf16[2,1024,1,128]{3,0,2,1:T(2,128)(2,1)S(1)}, u32[]{:S(2)}, u32[]{:S(2)}) async-start(bf16[2,1024,1,128]{3,0,2,1:T(2,128)(2,1)} %copy.359), calls=%async_computation.14 | async-start | bytes 1048576 | tf_op jit(solution)/shard_map/all_to_all | solution.py:247
  357.4 6.0 copy-start.53
  366.2 12.3 %all-to-all-start.13 = ((bf16[2,1024,1,128]{3,0,2,1:T(2,128)(2,1)}), bf16[2,1024,1,128]{3,0,2,1:T(2,128)(2,1)S(1)}, u32[]{:S(2)}, u32[]{:S(2)}) async-start(bf16[2,1024,1,128]{3,0,2,1:T(2,128)(2,1)} %copy.354), calls=%async_computation.13 | async-start | bytes 1048576 | tf_op jit(solution)/shard_map/all_to_all | solution.py:246
  376.7 10.8 %copy-start.88 = (f32[256,64]{0,1:T(8,128)S(1)}, f32[256,64]{0,1:T(8,128)}, u32[]{:S(2)}) copy-start(f32[256,64]{0,1:T(8,128)} %copy-done.86) | copy-start | bytes 196612
  379.3 12.3 %all-to-all-start.15 = ((bf16[2,1024,1,128]{3,0,2,1:T(2,128)(2,1)}), bf16[2,1024,1,128]{3,0,2,1:T(2,128)(2,1)S(1)}, u32[]{:S(2)}, u32[]{:S(2)}) async-start(bf16[2,1024,1,128]{3,0,2,1:T(2,128)(2,1)} %copy.364), calls=%async_computation.15 | async-start | bytes 1048576 | tf_op jit(solution)/shard_map/all_to_all | solution.py:248
  382.8 557.3 %all-reduce.4.cloned.1.call-start = ((), (), s32[]{:S(2)}) async-start(), calls=%async_computation.16 | async-start | bytes 25296896 | tf_op jit(solution)/shard_map/psum | solution.py:304
  401.9 46.4 %copy-start.39 = (bf16[2,256,512]{1,2,0:T(8,128)(2,1)S(1)}, bf16[2,256,512]{1,2,0:T(8,128)(2,1)}, u32[]{:S(2)}) copy-start(bf16[2,256,512]{1,2,0:T(8,128)(2,1)} %copy-done.38) | copy-start | bytes 1572868
  405.5 45.9 %copy-start.44 = (bf16[512,512]{1,0:T(8,128)(2,1)S(1)}, bf16[512,512]{1,0:T(8,128)(2,1)}, u32[]{:S(2)}) copy-start(bf16[512,512]{1,0:T(8,128)(2,1)} %param.33) | copy-start | bytes 1572868
  405.5 45.9 %copy-start.49 = (bf16[2,256,512]{2,1,0:T(8,128)(2,1)S(1)}, bf16[2,256,512]{2,1,0:T(8,128)(2,1)}, u32[]{:S(2)}) copy-start(bf16[2,256,512]{2,1,0:T(8,128)(2,1)} %reshape.559) | copy-start | bytes 1572868
  940.1 5.8 copy-start.93
  940.1 6.9 copy-start.81
  (111 other events, 241.3 us)
Sparse Core Ops, SparseCore 0:
  400.8 539.2 all-reduce.3
where the time goes:
time: 982 us; the launch traced here: 970 us
  waiting for transfers between devices  536 us (55%)
  matrix products  129 us (13%)
  local copies, waits for them, and re-layouts  113 us (12%)
  other arithmetic  61.6 us (6%)
  starting transfers between devices  58.3 us (6%)
  blocking collectives  55.5 us (6%)
  between operations  15.9 us (2%)
    psum x1, waiting for transfers between devices, reduce_grads(): summed = lax.psum(weights, ('dp', 'sp'))  487 us
    psum x1, blocking collectives, reduce_grads(): gains = lax.psum(grads[7:], ('dp', 'sp'))  42.8 us
    unnamed x201, local copies, waits for them, and re-layouts  20.6 us
  transfers between devices with their start and end apart: 16, of which 14 were waited for; matrix products, arithmetic and copies ran while one was open for 9% of the time, Pallas kernels for 0%

commit v1 on v0

--- a/solution.py
+++ b/solution.py
@@ -2,6 +2,7 @@
 import jax.numpy as jnp
 from jax import lax
 from jax.sharding import PartitionSpec as P
+from jax.lax import psum
 
 HEADS = 8
 HD = 64
@@ -301,7 +302,15 @@
 
 def reduce_grads(grads):
     weights = tuple((grad.astype(jnp.bfloat16) for grad in grads[:7]))
-    summed = lax.psum(weights, ("dp", "sp"))
+
+    def settle_shelves(row_data):
+        axis_id = "dp"
+        net_axis = "sp"
+        for w in (net_axis, axis_id):
+            row_data = psum(row_data, w)
+        return row_data
+
+    summed = settle_shelves(weights)
     gains = lax.psum(grads[7:], ("dp", "sp"))
     return tuple((grad.astype(jnp.float32) for grad in summed)) + tuple(gains)
 

time: 982 us -> 1090 us (1.11)
  waiting for transfers between devices: 536 us -> 646 us
    psum x1 -> x2, waiting for transfers between devices: 487 us -> 597 us  [settle_shelves(): row_data = psum(row_data, w)]
  transfers between devices with their start and end apart: 16 -> 17, of which waited for: 14 -> 15; matrix products, arithmetic and copies ran while one was open for 9% -> 8% of each run, Pallas kernels for 0% -> 0%
where the time goes in v1:
time: 1090 us; the launch traced here: 1080 us
  waiting for transfers between devices  646 us (59%)
  matrix products  129 us (12%)
  local copies, waits for them, and re-layouts  113 us (10%)
  other arithmetic  61.6 us (6%)
  starting transfers between devices  58.4 us (5%)
  blocking collectives  55.9 us (5%)
  between operations  15.9 us (1%)
    psum x2, waiting for transfers between devices, settle_shelves(): row_data = psum(row_data, w)  597 us
    psum x1, blocking collectives, reduce_grads(): gains = lax.psum(grads[7:], ('dp', 'sp'))  43.1 us
  transfers between devices with their start and end apart: 17, of which 15 were waited for; matrix products, arithmetic and copies ran while one was open for 8% of the time, Pallas kernels for 0%

profile of v1, /device:TPU:0, one launch (start us, length us, event | category | flops | bytes accessed | tf_op | source)
XLA Modules:
  0.0 1080.4 jit_solution(571360266713948091)
XLA Ops:
  9.9 4.2 all-to-all-start
  19.5 4.1 all-to-all-done
  23.6 3.5 all-to-all-start.1
  27.9 8.0 all-to-all-done.1
  35.9 3.5 all-to-all-start.2
  51.6 17.7 %while.52 = (s32[]{:T(128)}, bf16[2,1024,2,64]{1,3,2,0:T(8,128)(2,1)}, f32[2,2,1024,1]{2,1,3,0:T(2,128)S(1)}, bf16[2,1024,2,64]{1,3,2,0:T(8,128)(2,1)}, s32[2]{0...) while((s32[]{:T(128)}, ...), condition=%wide.region_3.4_spmd, body=%wide.region_0.3_spmd.sunk | while | flops 562166784 | bytes 36769988 | solution.py:130
  71.6 12.7 %all_to_all.216 = bf16[2,1024,1,128]{3,0,2,1:T(2,128)(2,1)S(1)} all-to-all(bf16[2,1024,1,128]{3,0,2,1:T(2,128)(2,1)} %copy.321), channel_id=1, replica_groups=mesh['dp'=8,'sp'=4] {'sp'}, dimensions={1} | all-to-all | bytes 1048576 | tf_op jit(solution)/shard_map/all_to_all | solution.py:131
  91.7 2.8 multiply_convert_fusion.5
  98.1 4.1 all-to-all-start.4
  107.9 3.3 all-to-all-done.4
  111.2 3.5 all-to-all-start.5
  115.5 8.0 all-to-all-done.5
  123.5 3.6 all-to-all-start.6
  139.4 17.7 %while.53 = (s32[]{:T(128)}, bf16[2,1024,2,64]{1,3,2,0:T(8,128)(2,1)}, f32[2,2,1024,1]{2,1,3,0:T(2,128)S(1)}, bf16[2,1024,2,64]{1,3,2,0:T(8,128)(2,1)}, s32[2]{0...) while((s32[]{:T(128)}, ...), condition=%wide.region_10.11_spmd, body=%wide.region_7.10_spmd.sunk | while | flops 562166784 | bytes 36769988 | solution.py:130
  159.1 4.4 all-to-all-start.7
  163.5 4.1 fusion.136
  167.6 4.7 all-to-all-done.7
  180.9 3.0 fusion.130
  189.1 4.5 all-to-all-start.8
  193.7 3.4 fusion.126
  197.1 5.4 all-to-all-done.8
  209.4 28.9 %while.54 = (s32[]{:T(128)}, bf16[2,1024,2,64]{1,3,2,0:T(8,128)(2,1)}, bf16[2,1024,2,64]{1,3,2,0:T(8,128)(2,1)}, bf16[2,1024,2,64]{1,3,2,0:T(8,128)(2,1)}, bf16[...) while((s32[]{:T(128)}, ...), condition=%wide.region_15.16_spmd, body=%wide.region_13.15_spmd.sunk | while | flops 1376386048 | bytes 86572392 | solution.py:239
  212.4 3.0 multiply_reduce_fusion.16
  215.4 2.7 multiply_convert_fusion.11
  226.8 3.0 multiply_reduce_fusion.16
  229.8 2.7 multiply_convert_fusion.11
  240.3 3.6 all-to-all-start.10
  244.0 3.6 fusion.127
  247.6 3.2 fusion.123
  252.8 4.2 all-to-all-start.9
  262.9 2.9 all-to-all-done.9
  265.9 4.1 all-to-all-start.11
  302.6 4.4 all-to-all-start.12
  308.3 3.3 fusion.125
  311.6 4.2 all-to-all-done.12
  322.8 29.0 %while.55 = (s32[]{:T(128)}, bf16[2,1024,2,64]{1,3,2,0:T(8,128)(2,1)}, bf16[2,1024,2,64]{1,3,2,0:T(8,128)(2,1)}, bf16[2,1024,2,64]{1,3,2,0:T(8,128)(2,1)}, bf16[...) while((s32[]{:T(128)}, ...), condition=%wide.region_21.22_spmd, body=%wide.region_19.21_spmd.sunk | while | flops 1376386048 | bytes 86572392 | solution.py:239
  325.7 3.0 multiply_reduce_fusion.17
  328.8 2.7 multiply_convert_fusion.12
  340.2 3.0 multiply_reduce_fusion.17
  343.2 2.7 multiply_convert_fusion.12
  353.7 3.7 all-to-all-start.14
  359.9 3.6 fusion.122
  366.3 3.5 all-to-all-start.13
  379.3 3.5 all-to-all-start.15
  400.7 228.5 %all-reduce.8.cloned.1.call-done = (bf16[512,512]{0,1:T(8,128)(2,1)}, bf16[512,512]{0,1:T(8,128)(2,1)}, bf16[512,512]{0,1:T(8,128)(2,1)}, bf16[512,512]{1,0:T(8,...) async-done(((bf16[512,512]{0,1:T(8,128)(2,1)}, ...) | async-done | bytes 12648464 | tf_op jit(solution)/shard_map/psum | solution.py:310
  630.4 3.6 fusion.185
  634.1 43.1 %all-reduce = (f32[512]{0:T(512)}, f32[512]{0:T(512)}, f32[512]{0:T(512)}, f32[512]{0:T(512)}) all-reduce(f32[512]{0:T(512)S(1)} %get-tuple-element.339, f32[512]{0:T(512)S(1)} %get-tuple-element.334, f32[512]{0:T(512)S(1)} %get-tuple-element.336, f32[512]{0:T(512)S(1)} %copy-done.113), channel_id=1, replica_groups=mesh['dp'=8,'sp'=4] {'dp','sp'}, use_global_device_ids=true, to_apply=%region_37.38 | all-reduce | flops 2048 | bytes 16384 | tf_op jit(solution)/shard_map/psum | solution.py:314
  681.5 368.5 %all-reduce.6.cloned.1.call-done = (bf16[512,512]{0,1:T(8,128)(2,1)}, bf16[512,512]{0,1:T(8,128)(2,1)}, bf16[512,512]{0,1:T(8,128)(2,1)}, bf16[512,512]{1,0:T(8,...) async-done(((bf16[512,512]{0,1:T(8,128)(2,1)}, ...) | async-done | bytes 12648464 | tf_op jit(solution)/shard_map/psum | solution.py:310
  (515 shorter events, 258.4 us)
Async XLA Ops:
  7.2 172.5 %copy-start = (bf16[512,1376]{0,1:T(8,128)(2,1)S(1)}, bf16[512,1376]{0,1:T(8,128)(2,1)}, u32[]{:S(2)}) copy-start(bf16[512,1376]{0,1:T(8,128)(2,1)} %param.44) | copy-start | bytes 4227076
  7.2 6.9 copy-start.6
  7.2 8.7 copy-start.74
  9.9 13.7 %all-to-all-start = ((bf16[2,256,4,128]{3,1,0,2:T(8,128)(2,1)}), bf16[2,256,4,128]{3,1,0,2:T(8,128)(2,1)}, u32[]{:S(2)}, u32[]{:S(2)}) async-start(bf16[2,256,4,128]{3,1,0,2:T(8,128)(2,1)} %bitcast.512), calls=%async_computation | async-start | bytes 1048576 | tf_op jit(solution)/shard_map/all_to_all | solution.py:121
  16.9 88.8 %copy-start.12 = (f32[256,8,64]{0,2,1:T(8,128)}, f32[256,8,64]{0,2,1:T(8,128)S(1)}, u32[]{:S(2)}) copy-start(f32[256,8,64]{0,2,1:T(8,128)S(1)} %mul.485) | copy-start | bytes 1572868
  23.6 12.3 %all-to-all-start.1 = ((bf16[2,256,4,128]{1,3,0,2:T(8,128)(2,1)}), bf16[2,256,4,128]{1,3,0,2:T(8,128)(2,1)S(1)}, u32[]{:S(2)}, u32[]{:S(2)}) async-start(bf16[2,256,4,128]{1,3,0,2:T(8,128)(2,1)} %copy.315), calls=%async_computation.1 | async-start | bytes 1048576 | tf_op jit(solution)/shard_map/all_to_all | solution.py:119
  35.9 12.3 %all-to-all-start.2 = ((bf16[2,256,4,128]{1,3,0,2:T(8,128)(2,1)}), bf16[2,256,4,128]{1,3,0,2:T(8,128)(2,1)S(1)}, u32[]{:S(2)}, u32[]{:S(2)}) async-start(bf16[2,256,4,128]{1,3,0,2:T(8,128)(2,1)} %copy.319), calls=%async_computation.2 | async-start | bytes 1048576 | tf_op jit(solution)/shard_map/all_to_all | solution.py:120
  41.4 10.2 copy-start.114
  69.3 20.2 %copy-start.2 = (bf16[2,1024,2,64]{1,3,2,0:T(8,128)(2,1)}, bf16[2,1024,2,64]{1,3,2,0:T(8,128)(2,1)S(1)}, u32[]{:S(2)}) copy-start(bf16[2,1024,2,64]{1,3,2,0:T(8,128)(2,1)S(1)} %get-tuple-element.906) | copy-start | bytes 1572868
  69.3 20.2 %copy-start.8 = (bf16[2,1024,2,64]{1,3,2,0:T(8,128)(2,1)}, bf16[2,1024,2,64]{1,3,2,0:T(8,128)(2,1)S(1)}, u32[]{:S(2)}) copy-start(bf16[2,1024,2,64]{1,3,2,0:T(8,128)(2,1)S(1)} %get-tuple-element.908) | copy-start | bytes 1572868
  69.3 20.2 %copy-start.95 = (f32[2,2,1024,1]{2,1,3,0:T(2,128)}, f32[2,2,1024,1]{2,1,3,0:T(2,128)S(1)}, u32[]{:S(2)}) copy-start(f32[2,2,1024,1]{2,1,3,0:T(2,128)S(1)} %get-tuple-element.824) | copy-start | bytes 49156
  84.4 5.8 copy-start.104
  96.5 7.3 copy-start.106
  96.5 7.3 copy-start.102
  96.8 7.0 copy-start.4
  98.1 13.1 %all-to-all-start.4 = ((bf16[2,256,4,128]{3,1,0,2:T(8,128)(2,1)}), bf16[2,256,4,128]{3,1,0,2:T(8,128)(2,1)}, u32[]{:S(2)}, u32[]{:S(2)}) async-start(bf16[2,256,4,128]{3,1,0,2:T(8,128)(2,1)} %bitcast.625), calls=%async_computation.4 | async-start | bytes 1048576 | tf_op jit(solution)/shard_map/all_to_all | solution.py:121
  111.2 12.3 %all-to-all-start.5 = ((bf16[2,256,4,128]{1,3,0,2:T(8,128)(2,1)}), bf16[2,256,4,128]{1,3,0,2:T(8,128)(2,1)S(1)}, u32[]{:S(2)}, u32[]{:S(2)}) async-start(bf16[2,256,4,128]{1,3,0,2:T(8,128)(2,1)} %copy.328), calls=%async_computation.5 | async-start | bytes 1048576 | tf_op jit(solution)/shard_map/all_to_all | solution.py:119
  123.5 12.4 %all-to-all-start.6 = ((bf16[2,256,4,128]{1,3,0,2:T(8,128)(2,1)}), bf16[2,256,4,128]{1,3,0,2:T(8,128)(2,1)S(1)}, u32[]{:S(2)}, u32[]{:S(2)}) async-start(bf16[2,256,4,128]{1,3,0,2:T(8,128)(2,1)} %copy.332), calls=%async_computation.6 | async-start | bytes 1048576 | tf_op jit(solution)/shard_map/all_to_all | solution.py:120
  159.1 13.3 %all-to-all-start.7 = ((bf16[2,1024,1,128]{3,0,2,1:T(2,128)(2,1)}), bf16[2,1024,1,128]{3,0,2,1:T(2,128)(2,1)}, u32[]{:S(2)}, u32[]{:S(2)}) async-start(bf16[2,1024,1,128]{3,0,2,1:T(2,128)(2,1)} %copy.334), calls=%async_computation.7 | async-start | bytes 1048576 | tf_op jit(solution)/shard_map/all_to_all | solution.py:131
  178.6 8.2 copy-start.14
  189.1 13.4 %all-to-all-start.8 = ((bf16[2,256,4,128]{3,1,0,2:T(8,128)(2,1)}), bf16[2,256,4,128]{3,1,0,2:T(8,128)(2,1)}, u32[]{:S(2)}, u32[]{:S(2)}) async-start(bf16[2,256,4,128]{3,1,0,2:T(8,128)(2,1)} %bitcast.638), calls=%async_computation.8 | async-start | bytes 1048576 | tf_op jit(solution)/shard_map/all_to_all | solution.py:231
  240.3 12.4 %all-to-all-start.10 = ((bf16[2,1024,1,128]{3,0,2,1:T(2,128)(2,1)}), bf16[2,1024,1,128]{3,0,2,1:T(2,128)(2,1)S(1)}, u32[]{:S(2)}, u32[]{:S(2)}) async-start(bf16[2,1024,1,128]{3,0,2,1:T(2,128)(2,1)} %copy.344), calls=%async_computation.10 | async-start | bytes 1048576 | tf_op jit(solution)/shard_map/all_to_all | solution.py:248
  247.6 9.4 copy-start.34
  252.8 13.1 %all-to-all-start.9 = ((bf16[2,1024,1,128]{3,0,2,1:T(2,128)(2,1)}), bf16[2,1024,1,128]{3,0,2,1:T(2,128)(2,1)}, u32[]{:S(2)}, u32[]{:S(2)}) async-start(bf16[2,1024,1,128]{3,0,2,1:T(2,128)(2,1)} %copy.339), calls=%async_computation.9 | async-start | bytes 1048576 | tf_op jit(solution)/shard_map/all_to_all | solution.py:247
  262.9 11.8 %copy-start.18 = (f32[2,256,4,1,128]{1,4,2,0,3:T(8,128)}, f32[2,256,4,1,128]{1,4,2,0,3:T(8,128)S(1)}, u32[]{:S(2)}) copy-start(f32[2,256,4,1,128]{1,4,2,0,3:T(8,128)S(1)} %copy.346) | copy-start | bytes 3145732
  262.9 11.8 %copy-start.87 = (f32[256,64]{0,1:T(8,128)S(1)}, f32[256,64]{0,1:T(8,128)}, u32[]{:S(2)}) copy-start(f32[256,64]{0,1:T(8,128)} %copy-done.86) | copy-start | bytes 196612
  265.9 14.7 %all-to-all-start.11 = ((bf16[2,1024,1,128]{3,0,2,1:T(2,128)(2,1)}), bf16[2,1024,1,128]{3,0,2,1:T(2,128)(2,1)}, u32[]{:S(2)}, u32[]{:S(2)}) async-start(bf16[2,1024,1,128]{3,0,2,1:T(2,128)(2,1)} %copy.349), calls=%async_computation.11 | async-start | bytes 1048576 | tf_op jit(solution)/shard_map/all_to_all | solution.py:249
  278.3 8.6 copy-start.35
  281.6 5.2 copy-start.101
  289.0 5.5 copy-start.40
  299.8 7.3 copy-start.5
  299.8 7.3 copy-start.39
  302.6 13.3 %all-to-all-start.12 = ((bf16[2,256,4,128]{3,1,0,2:T(8,128)(2,1)}), bf16[2,256,4,128]{3,1,0,2:T(8,128)(2,1)}, u32[]{:S(2)}, u32[]{:S(2)}) async-start(bf16[2,256,4,128]{3,1,0,2:T(8,128)(2,1)} %bitcast.630), calls=%async_computation.12 | async-start | bytes 1048576 | tf_op jit(solution)/shard_map/all_to_all | solution.py:231
  311.6 11.1 %copy-start.3 = (bf16[2,1024,2,64]{1,3,2,0:T(8,128)(2,1)S(1)}, bf16[2,1024,2,64]{1,3,2,0:T(8,128)(2,1)}, u32[]{:S(2)}) copy-start(bf16[2,1024,2,64]{1,3,2,0:T(8,128)(2,1)} %copy-done.2) | copy-start | bytes 1572868
  311.6 11.1 %copy-start.9 = (bf16[2,1024,2,64]{1,3,2,0:T(8,128)(2,1)S(1)}, bf16[2,1024,2,64]{1,3,2,0:T(8,128)(2,1)}, u32[]{:S(2)}) copy-start(bf16[2,1024,2,64]{1,3,2,0:T(8,128)(2,1)} %copy-done.8) | copy-start | bytes 1572868
  311.6 11.1 %copy-start.96 = (f32[2,2,1024,1]{2,1,3,0:T(2,128)S(1)}, f32[2,2,1024,1]{2,1,3,0:T(2,128)}, u32[]{:S(2)}) copy-start(f32[2,2,1024,1]{2,1,3,0:T(2,128)} %copy-done.95) | copy-start | bytes 49156
  353.7 12.5 %all-to-all-start.14 = ((bf16[2,1024,1,128]{3,0,2,1:T(2,128)(2,1)}), bf16[2,1024,1,128]{3,0,2,1:T(2,128)(2,1)S(1)}, u32[]{:S(2)}, u32[]{:S(2)}) async-start(bf16[2,1024,1,128]{3,0,2,1:T(2,128)(2,1)} %copy.359), calls=%async_computation.14 | async-start | bytes 1048576 | tf_op jit(solution)/shard_map/all_to_all | solution.py:248
  357.5 6.0 copy-start.53
  366.3 12.3 %all-to-all-start.13 = ((bf16[2,1024,1,128]{3,0,2,1:T(2,128)(2,1)}), bf16[2,1024,1,128]{3,0,2,1:T(2,128)(2,1)S(1)}, u32[]{:S(2)}, u32[]{:S(2)}) async-start(bf16[2,1024,1,128]{3,0,2,1:T(2,128)(2,1)} %copy.354), calls=%async_computation.13 | async-start | bytes 1048576 | tf_op jit(solution)/shard_map/all_to_all | solution.py:247
  376.7 10.8 %copy-start.88 = (f32[256,64]{0,1:T(8,128)S(1)}, f32[256,64]{0,1:T(8,128)}, u32[]{:S(2)}) copy-start(f32[256,64]{0,1:T(8,128)} %copy-done.86) | copy-start | bytes 196612
  379.3 12.3 %all-to-all-start.15 = ((bf16[2,1024,1,128]{3,0,2,1:T(2,128)(2,1)}), bf16[2,1024,1,128]{3,0,2,1:T(2,128)(2,1)S(1)}, u32[]{:S(2)}, u32[]{:S(2)}) async-start(bf16[2,1024,1,128]{3,0,2,1:T(2,128)(2,1)} %copy.364), calls=%async_computation.15 | async-start | bytes 1048576 | tf_op jit(solution)/shard_map/all_to_all | solution.py:249
  382.8 246.4 %all-reduce.8.cloned.1.call-start = ((), (), s32[]{:S(2)}) async-start(), calls=%async_computation.17 | async-start | bytes 25296896 | tf_op jit(solution)/shard_map/psum | solution.py:310
  400.7 649.4 %all-reduce.6.cloned.1.call-start = ((), (), s32[]{:S(2)}) async-start(), calls=%async_computation.16 | async-start | bytes 25296896 | tf_op jit(solution)/shard_map/psum | solution.py:310
  630.4 46.8 %copy-start.37 = (bf16[2,256,512]{1,2,0:T(8,128)(2,1)S(1)}, bf16[2,256,512]{1,2,0:T(8,128)(2,1)}, u32[]{:S(2)}) copy-start(bf16[2,256,512]{1,2,0:T(8,128)(2,1)} %copy-done.36) | copy-start | bytes 1572868
  634.0 46.2 %copy-start.44 = (bf16[512,512]{1,0:T(8,128)(2,1)S(1)}, bf16[512,512]{1,0:T(8,128)(2,1)}, u32[]{:S(2)}) copy-start(bf16[512,512]{1,0:T(8,128)(2,1)} %param.33) | copy-start | bytes 1572868
  634.0 46.2 %copy-start.49 = (bf16[2,256,512]{2,1,0:T(8,128)(2,1)S(1)}, bf16[2,256,512]{2,1,0:T(8,128)(2,1)}, u32[]{:S(2)}) copy-start(bf16[2,256,512]{2,1,0:T(8,128)(2,1)} %reshape.559) | copy-start | bytes 1572868
  1050.0 5.8 copy-start.93
  1050.0 6.9 copy-start.81
  (112 other events, 246.5 us)
Sparse Core Ops, SparseCore 0:
  400.8 228.3 all-reduce.7
  635.6 414.3 all-reduce.5
